TPU v7x, 512 devices: a whole 4x8x8 slice. The times are simulated.
512 devices in a mesh: lon: 32 (over x, y_hi, core), head: 16 (over z, y_lo).
Axes of the slice: x: 4, y: 8 (y_hi: 4, y_lo: 2; y = y_hi * 2 + y_lo), z: 8, core: 2. Of those that a mesh axis runs over, the one named last changes fastest.
Arguments:
- latents: bfloat16 [3, 48, 256, 1024], P(None, 'head', 'lon'), may hold values from -16 to 16
- out_grad: bfloat16 [3, 48, 256, 1024], P(None, 'head', 'lon'), may hold values from -6 to 6
- qkv_weight: bfloat16 [16, 1024, 192], P('head'), as said below
- out_weight: bfloat16 [16, 64, 1024], replicated, may hold values from -0.1875 to 0.1875
Outputs:
- mixed: bfloat16 [3, 48, 256, 1024], P(None, 'head', 'lon')
- latent_grad: bfloat16 [3, 48, 256, 1024], P(None, 'head', 'lon')
- qkv_grad: float32 [16, 1024, 192], P('head')
Inputs may be any that keep to these rules, and one draw needn't show every extreme that they name: `qkv_weight`: entries lie within -14 / sqrt(1024) and 14 / sqrt(1024).
All inputs are finite; a program needn't handle non-finite values.
Results may differ from a plain program's by a relative error of at most 0.024.
The roundings to bfloat16 on the way count: a program that leaves them out, or rounds other values in their place, can miss the bound.
Values may be sent and summed in bfloat16 or wider, within the bound.
No kernel may reach another device: no remote copies, remote signals or barrier semaphores. Data moves between devices by JAX's collectives and lax.ppermute only.
A program may use at most 64 MiB of HBM per device.

v0:
```python
import jax
import jax.numpy as jnp
from jax import lax
from jax.sharding import PartitionSpec as P

WIN_LAT = 6
WIN_LON = 8
MASKED = -1e30


def extended(block, sides, width):
    for axis, dim in sides:
        count = lax.axis_size(axis)
        forward = [(i, i + 1) for i in range(count - 1)]
        forward.append((count - 1, 0))
        backward = [(target, source) for source, target in forward]
        low = lax.ppermute(
            lax.slice_in_dim(block, block.shape[dim] - width, None, axis=dim), axis, forward
        )
        high = lax.ppermute(lax.slice_in_dim(block, 0, width, axis=dim), axis, backward)
        block = jnp.concatenate([low, block, high], axis=dim)
    return block


def shifted(block, axis, distance):
    devices = range(lax.axis_size(axis))
    route = [((i - distance) % len(devices), i) for i in devices]
    return lax.ppermute(block, axis, route)


def softmax_rows(query_rows, key_rows, valid, score_scale_factor):
    score_matrix = (
        jnp.einsum("fud,fwd->fuw", query_rows, key_rows, preferred_element_type=jnp.float32)
        * score_scale_factor
    )
    score_matrix = jnp.where(valid[:, None, :], score_matrix, MASKED)
    row_max = jnp.max(score_matrix, axis=-1, keepdims=True)
    powers = jnp.exp(score_matrix - row_max)
    return powers / jnp.sum(powers, axis=-1, keepdims=True)


def attend_block(pack, head_width, score_scale_factor):
    query_rows, key_value_pairs, valid = pack
    probs = softmax_rows(query_rows, key_value_pairs[..., :head_width], valid, score_scale_factor)
    probabilities_bfloat = probs.astype(jnp.bfloat16)
    attended_values = jnp.einsum(
        "ucf,ufg->ucg",
        probabilities_bfloat,
        key_value_pairs[..., head_width:],
        preferred_element_type=jnp.float32,
    )
    return attended_values.astype(jnp.bfloat16)


def attend_grad(pack, head_width, score_scale_factor):
    query_rows, key_value_pairs, valid, outer_gradient = pack
    key_portion = key_value_pairs[..., :head_width]
    value_portion = key_value_pairs[..., head_width:]
    probs = softmax_rows(query_rows, key_portion, valid, score_scale_factor)
    probabilities_bfloat = probs.astype(jnp.bfloat16)
    probability_gradient = jnp.einsum(
        "fud,fwd->fuw", outer_gradient, value_portion, preferred_element_type=jnp.float32
    )
    centre = jnp.sum(probs * probability_gradient, axis=-1, keepdims=True)
    score_gradient = (probs * (probability_gradient - centre)).astype(jnp.bfloat16)
    query_gradient = (
        jnp.einsum("ucf,ufg->ucg", score_gradient, key_portion, preferred_element_type=jnp.float32)
        * score_scale_factor
    )
    key_gradient = (
        jnp.einsum("txd,txr->tdr", score_gradient, query_rows, preferred_element_type=jnp.float32)
        * score_scale_factor
    )
    value_gradient = jnp.einsum(
        "txd,txr->tdr", probabilities_bfloat, outer_gradient, preferred_element_type=jnp.float32
    )
    return (query_gradient, jnp.concatenate([key_gradient, value_gradient], axis=-1))


def window_rows(values, windows):
    levels, lat_rows, columns, per_dev, inner = values.shape
    shaped = values.reshape(levels, windows, WIN_LAT, columns, per_dev, inner)
    return shaped.transpose(4, 1, 0, 2, 3, 5).reshape(
        per_dev * windows, levels * WIN_LAT * columns, inner
    )


def unwindow_rows(values, levels, windows, columns, per_dev):
    inner = values.shape[-1]
    shaped = values.reshape(per_dev, windows, levels, WIN_LAT, columns, inner).transpose(
        2, 1, 3, 4, 0, 5
    )
    return shaped.reshape(levels, windows * WIN_LAT, columns, per_dev, inner)


def window_keys(kv_ext, windows):
    levels, lat_rows, key_cols, per_dev, inner = kv_ext.shape
    half_lat = WIN_LAT // 2
    padded = jnp.pad(kv_ext, ((0, 0), (half_lat, half_lat), (0, 0), (0, 0), (0, 0)))
    lower = padded[:, :lat_rows].reshape(levels, windows, WIN_LAT, key_cols, per_dev, inner)
    upper = padded[:, WIN_LAT : lat_rows + WIN_LAT].reshape(
        levels, windows, WIN_LAT, key_cols, per_dev, inner
    )
    joined = jnp.concatenate([lower, upper], axis=2)
    return joined.transpose(4, 1, 0, 2, 3, 5).reshape(
        per_dev * windows, levels * 2 * WIN_LAT * key_cols, inner
    )


def unwindow_keys(grads, levels, windows, key_cols, per_dev):
    inner = grads.shape[-1]
    lat_rows = windows * WIN_LAT
    half_lat = WIN_LAT // 2
    shaped = grads.reshape(per_dev, windows, levels, 2 * WIN_LAT, key_cols, inner).transpose(
        2, 1, 3, 4, 0, 5
    )
    lower = shaped[:, :, :WIN_LAT].reshape(levels, lat_rows, key_cols, per_dev, inner)
    upper = shaped[:, :, WIN_LAT:].reshape(levels, lat_rows, key_cols, per_dev, inner)
    summed = jnp.pad(lower, ((0, 0), (0, WIN_LAT), (0, 0), (0, 0), (0, 0))) + jnp.pad(
        upper, ((0, 0), (WIN_LAT, 0), (0, 0), (0, 0), (0, 0))
    )
    return summed[:, half_lat : half_lat + lat_rows]


def key_valid(levels, windows, key_cols, per_dev, lat_rows):
    lat_index = (
        WIN_LAT * jnp.arange(windows)[:, None] - WIN_LAT // 2 + jnp.arange(2 * WIN_LAT)[None, :]
    )
    inside = (lat_index >= 0) & (lat_index < lat_rows)
    spread = jnp.broadcast_to(
        inside[None, :, None, :, None], (per_dev, windows, levels, 2 * WIN_LAT, key_cols)
    )
    return spread.reshape(per_dev * windows, -1)


def to_blocks(values):
    return values.reshape((values.shape[0] // 4, 4) + values.shape[1:])


def from_blocks(values):
    return values.reshape((-1,) + values.shape[2:])


def body(latents, out_grad, qkv_weight, out_weight):
    levels, lat_dev, columns, model_width = latents.shape
    groups = lax.axis_size("head")
    lat_rows = lat_dev * groups
    per_dev = qkv_weight.shape[0]
    head_count = out_weight.shape[0]
    head_width = out_weight.shape[1]
    score_scale_factor = head_width ** (-0.5)
    windows = lat_rows // WIN_LAT
    half_lon = WIN_LON // 2
    out_flat = out_weight.reshape(head_count * head_width, model_width)
    band_rows = lax.all_gather(latents, "head", axis=1, tiled=True)
    projected = jnp.einsum(
        "lawd,hdc->lawhc", band_rows, qkv_weight, preferred_element_type=jnp.float32
    ).astype(jnp.bfloat16)
    kv_ext = extended(projected[..., head_width:], (("lon", 2),), half_lon)
    key_cols = kv_ext.shape[2]
    query_rows = window_rows(projected[..., :head_width], windows)
    key_value_pairs = window_keys(kv_ext, windows)
    valid = key_valid(levels, windows, key_cols, per_dev, lat_rows)
    attended_values = lax.map(
        lambda pack: attend_block(pack, head_width, score_scale_factor),
        (to_blocks(query_rows), to_blocks(key_value_pairs), to_blocks(valid)),
    )
    attended_values = unwindow_rows(from_blocks(attended_values), levels, windows, columns, per_dev)
    attended_values = attended_values.reshape(levels, lat_rows, columns, per_dev * head_width)
    token_attended = lax.all_to_all(
        attended_values, "head", split_axis=1, concat_axis=3, tiled=True
    )
    mixed = jnp.dot(
        token_attended.reshape(-1, head_count * head_width),
        out_flat,
        preferred_element_type=jnp.float32,
    )
    mixed = mixed.astype(jnp.bfloat16).reshape(latents.shape)
    token_grad = jnp.dot(
        out_grad.reshape(-1, model_width), out_flat.T, preferred_element_type=jnp.float32
    ).astype(jnp.bfloat16)
    token_grad = token_grad.reshape(levels, lat_dev, columns, head_count * head_width)
    band_grad = lax.all_to_all(token_grad, "head", split_axis=3, concat_axis=1, tiled=True)
    band_grad = window_rows(
        band_grad.reshape(levels, lat_rows, columns, per_dev, head_width), windows
    )
    query_gradient, pair_grad = lax.map(
        lambda pack: attend_grad(pack, head_width, score_scale_factor),
        (to_blocks(query_rows), to_blocks(key_value_pairs), to_blocks(valid), to_blocks(band_grad)),
    )
    query_gradient = unwindow_rows(from_blocks(query_gradient), levels, windows, columns, per_dev)
    ext_grad = unwindow_keys(from_blocks(pair_grad), levels, windows, key_cols, per_dev)
    west_edge = ext_grad[:, :, half_lon + columns :].astype(jnp.bfloat16)
    east_edge = ext_grad[:, :, :half_lon].astype(jnp.bfloat16)
    from_west = shifted(west_edge, "lon", 1).astype(jnp.float32)
    from_east = shifted(east_edge, "lon", -1).astype(jnp.float32)
    own_grad = ext_grad[:, :, half_lon : half_lon + columns]
    own_grad = own_grad + jnp.pad(
        from_west, ((0, 0), (0, 0), (0, columns - half_lon), (0, 0), (0, 0))
    )
    own_grad = own_grad + jnp.pad(
        from_east, ((0, 0), (0, 0), (columns - half_lon, 0), (0, 0), (0, 0))
    )
    projected_grad = jnp.concatenate([query_gradient, own_grad], axis=-1).astype(jnp.bfloat16)
    grad_tokens = lax.all_to_all(
        projected_grad.reshape(levels, lat_rows, columns, per_dev * 3 * head_width),
        "head",
        split_axis=1,
        concat_axis=3,
        tiled=True,
    )
    grad_flat = grad_tokens.reshape(-1, head_count * 3 * head_width)
    piece = lax.all_gather(qkv_weight, "head", axis=0, tiled=True)
    part_cols = grad_flat
    part_cols = part_cols.reshape(grad_flat.shape[0], piece.shape[0], 3 * head_width)
    latent_sum = jnp.einsum("rnc,ndc->rd", part_cols, piece, preferred_element_type=jnp.float32)
    local_grad = jnp.einsum(
        "lawd,lawhc->hdc", band_rows, projected_grad, preferred_element_type=jnp.float32
    )
    latent_grad = latent_sum.astype(jnp.bfloat16).reshape(latents.shape)
    qkv_grad = lax.psum(local_grad.astype(jnp.bfloat16), "lon").astype(jnp.float32)
    return (mixed, latent_grad, qkv_grad)


def solution(mesh):
    placed = (
        P(None, "head", "lon", None),
        P(None, "head", "lon", None),
        P("head", None, None),
        P(),
    )
    return jax.shard_map(
        body,
        mesh=mesh,
        in_specs=placed,
        out_specs=(
            P(None, "head", "lon", None),
            P(None, "head", "lon", None),
            P("head", None, None),
        ),
        check_vma=False,
    )
```

profile of v0, /device:TPU:1, one launch (start us, length us, event | category | flops | bytes accessed | tf_op | source)
XLA Modules:
  0.0 604.0 jit_solution(525923004497261333)
XLA Ops:
  10.4 3.6 copy.69
  14.1 5.8 reshape.129
  19.9 12.0 %all-to-all-start.1 = ((bf16[16,2,2304]{2,1,0:T(2,128)(2,1)}), bf16[16,2,2304]{2,1,0:T(2,128)(2,1)S(1)}, u32[]{:S(2)}, u32[]{:S(2)}) async-start(bf16[16,2,2304]{2,1,0:T(2,128)(2,1)} %reshape.129), calls=%async_computation.1 | async-start | bytes 294912 | tf_op jit(solution)/shard_map/all_to_all | solution.py:183
  31.9 54.7 %all-gather.3.cloned.1.call-done = bf16[3,48,8,1024]{3,2,1,0:T(8,128)(2,1)} async-done(((bf16[3,3,8,1024]{3,2,1,0:T(8,128)(2,1)}), bf16[3,48,8,1024]{3,2,1,0:T(8,128)(2,1)}) %all-gather.3.cloned.1.call-update) | async-done | bytes 2359312 | tf_op jit(solution)/shard_map/all_gather | solution.py:155
  90.1 11.9 %collective-permute-start.1 = (bf16[3,48,4,1,128]{4,2,1,0,3:T(4,128)(2,1)}, bf16[3,48,4,1,128]{4,2,1,0,3:T(4,128)(2,1)}, u32[]{:S(2)}, u32[]{:S(2)}) collective-permute-start(bf16[3,48,4,1,128]{4,2,1,0,3:T(4,128)(2,1)} %get-tuple-element.142), channel_id=1, source_target_pairs={{16,0},{32,16},{48,32},{64,48},{80,64},{96,80},{112,96},{128,112},... | collective-permute-start | bytes 442376 | tf_op jit(solution)/shard_map/ppermute | solution.py:20
  102.0 3.8 collective-permute-start
  106.2 3.9 reshape.130
  110.1 3.9 copy.92
  120.7 26.0 %while.23 = (s32[]{:T(128)}, bf16[2,4,144,64]{2,3,1,0:T(8,128)(2,1)}, f32[2,4,576,128]{3,2,1,0:T(8,128)}, pred[2,4,576]{2,1,0:T(4,128)(4,1)S(1)}, bf16[2,4,144,6...) while((s32[]{:T(128)}, ...), condition=%wide.region_8.9_spmd, body=%wide.region_4.8_spmd.sunk | while | flops 217128960 | bytes 40974684 | solution.py:187
  121.7 2.9 fusion.162
  131.2 2.5 constant_dynamic-update-slice_fusion.2
  134.7 2.9 fusion.162
  144.2 2.5 constant_dynamic-update-slice_fusion.2
  153.7 4.7 collective-permute-start.2
  163.9 2.7 fusion.88
  167.4 11.0 %while.22 = (s32[]{:T(128)}, bf16[2,4,144,64]{2,3,1,0:T(8,128)(2,1)}, pred[2,4,576]{2,1,0:T(4,128)(4,1)S(1)}, bf16[2,4,144,64]{2,3,1,0:T(8,128)(2,1)}, bf16[2,4,576,128]{2,3,1,0:T(8,128)(2,1)S(1)}, /*index=5*/s32[]{:T(128)}) while((s32[]{:T(128)}, bf16[2,4,144,64]{2,3,1,0:T(8,128)(2,1)}, pred[2,4,576]{2,1,0:T(4,128)(4,1)S(1)}, ...), condition=%wide.region_3.4_spmd, body=%wide.region_0.3_spmd.sunk | while | flops 130426560 | bytes 2570841 | solution.py:164
  170.2 2.7 fusion.153
  175.6 2.7 fusion.153
  180.5 4.3 all-to-all-start
  186.1 6.7 %all-to-all-done = bf16[16,2,2304]{2,1,0:T(2,128)(2,1)S(1)} async-done(((bf16[16,2,2304]{2,1,0:T(2,128)(2,1)}), bf16[16,2,2304]{2,1,0:T(2,128)(2,1)S(1)}, u32[]{:S(2)}, u32[]{:S(2)}) %all-to-all-start) | async-done | bytes 147488 | tf_op jit(solution)/shard_map/all_to_all | solution.py:170
  192.8 3.6 all-to-all-start.2
  198.0 249.5 %all-reduce.7.cloned.1.call-done = bf16[1,1024,192]{1,2,0:T(8,128)(2,1)} async-done(((bf16[1,1024,192]{1,2,0:T(8,128)(2,1)}), bf16[1,1024,192]{1,2,0:T(8,128)(2,1)}) %all-reduce.7.cloned.1.call-update) | async-done | bytes 393232 | tf_op jit(solution)/shard_map/psum | solution.py:221
  449.5 143.2 %all-gather.5.cloned.1.call-done = bf16[16,1024,192]{1,2,0:T(8,128)(2,1)} async-done(((bf16[1,1024,192]{1,2,0:T(8,128)(2,1)}), bf16[16,1024,192]{1,2,0:T(8,128)(2,1)}) %all-gather.5.cloned.1.call-update) | async-done | bytes 6291472 | tf_op jit(solution)/shard_map/all_gather | solution.py:213
  592.8 4.7 fusion.91
  (133 shorter events, 54.5 us)
Async XLA Ops:
  7.2 1.6 copy-start
  7.2 79.4 %all-gather.3.cloned.1.call-start = ((), (), s32[]{:S(2)}) async-start(), calls=%async_computation.3 | async-start | bytes 2506752 | tf_op jit(solution)/shard_map/all_gather | solution.py:155
  14.1 72.5 %copy-start.13 = (bf16[1,1024,192]{1,2,0:T(8,128)(2,1)S(1)}, bf16[1,1024,192]{1,2,0:T(8,128)(2,1)}, u32[]{:S(2)}) copy-start(bf16[1,1024,192]{1,2,0:T(8,128)(2,1)} %param.10) | copy-start | bytes 1179652
  19.9 86.3 %all-to-all-start.1 = ((bf16[16,2,2304]{2,1,0:T(2,128)(2,1)}), bf16[16,2,2304]{2,1,0:T(2,128)(2,1)S(1)}, u32[]{:S(2)}, u32[]{:S(2)}) async-start(bf16[16,2,2304]{2,1,0:T(2,128)(2,1)} %reshape.129), calls=%async_computation.1 | async-start | bytes 294912 | tf_op jit(solution)/shard_map/all_to_all | solution.py:183
  31.8 415.7 %all-reduce.7.cloned.1.call-start = ((), (), s32[]{:S(2)}) async-start(), calls=%async_computation.5 | async-start | bytes 786432 | tf_op jit(solution)/shard_map/psum | solution.py:221
  90.1 26.0 %collective-permute-start.1 = (bf16[3,48,4,1,128]{4,2,1,0,3:T(4,128)(2,1)}, bf16[3,48,4,1,128]{4,2,1,0,3:T(4,128)(2,1)}, u32[]{:S(2)}, u32[]{:S(2)}) collective-permute-start(bf16[3,48,4,1,128]{4,2,1,0,3:T(4,128)(2,1)} %get-tuple-element.142), channel_id=1, source_target_pairs={{16,0},{32,16},{48,32},{64,48},{80,64},{96,80},{112,96},{128,112},... | collective-permute-start | bytes 442376 | tf_op jit(solution)/shard_map/ppermute | solution.py:20
  102.0 14.1 %collective-permute-start = (bf16[3,48,4,1,128]{4,2,1,0,3:T(4,128)(2,1)}, bf16[3,48,4,1,128]{4,2,1,0,3:T(4,128)(2,1)}, u32[]{:S(2)}, u32[]{:S(2)}) collective-permute-start(bf16[3,48,4,1,128]{4,2,1,0,3:T(4,128)(2,1)} %get-tuple-element.141), channel_id=1, source_target_pairs={{0,16},{16,32},{32,48},{48,64},{64,80},{80,96},{96,112},{112,128},... | collective-permute-start | bytes 442376 | tf_op jit(solution)/shard_map/ppermute | solution.py:17
  120.7 3.9 copy-start.1
  124.6 2.2 copy-start.3
  126.8 1.6 copy-start.14
  131.2 2.5 copy-start.2
  133.7 3.9 copy-start.1
  137.6 2.2 copy-start.3
  139.8 1.6 copy-start.14
  144.2 2.5 copy-start.2
  151.8 9.6 %collective-permute-start.3 = (bf16[3,48,4,1,128]{4,1,2,0,3:T(8,128)(2,1)}, bf16[3,48,4,1,128]{4,1,2,0,3:T(8,128)(2,1)}, u32[]{:S(2)}, u32[]{:S(2)}) collective-permute-start(bf16[3,48,4,1,128]{4,1,2,0,3:T(8,128)(2,1)} %get-tuple-element.138), channel_id=1, source_target_pairs={{16,0},{32,16},{48,32},{64,48},{80,64},{96,80},{112,96},{128,112},... | collective-permute-start | bytes 442376 | tf_op jit(solution)/shard_map/ppermute | solution.py:28
  153.7 7.7 %collective-permute-start.2 = (bf16[3,48,4,1,128]{4,1,2,0,3:T(8,128)(2,1)}, bf16[3,48,4,1,128]{4,1,2,0,3:T(8,128)(2,1)}, u32[]{:S(2)}, u32[]{:S(2)}) collective-permute-start(bf16[3,48,4,1,128]{4,1,2,0,3:T(8,128)(2,1)} %get-tuple-element.137), channel_id=1, source_target_pairs={{496,0},{0,16},{16,32},{32,48},{48,64},{64,80},{80,96},{96,112},{1... | collective-permute-start | bytes 442376 | tf_op jit(solution)/shard_map/ppermute | solution.py:28
  161.4 1.8 copy-start.11
  161.4 2.5 copy-start.17
  166.6 426.1 %all-gather.5.cloned.1.call-start = ((), (), s32[]{:S(2)}) async-start(), calls=%async_computation.4 | async-start | bytes 6684672 | tf_op jit(solution)/shard_map/all_gather | solution.py:213
  178.3 6.4 %copy-start.10 = (bf16[3,48,8,128]{3,1,2,0:T(8,128)(2,1)S(1)}, bf16[3,48,8,128]{3,1,2,0:T(8,128)(2,1)}, u32[]{:S(2)}) copy-start(bf16[3,48,8,128]{3,1,2,0:T(8,128)(2,1)} %copy-done.9) | copy-start | bytes 884740
  178.3 6.5 %copy-start.12 = (bf16[3,48,8,64]{3,1,2,0:T(8,128)(2,1)S(1)}, bf16[3,48,8,64]{3,1,2,0:T(8,128)(2,1)}, u32[]{:S(2)}) copy-start(bf16[3,48,8,64]{3,1,2,0:T(8,128)(2,1)} %copy-done.11) | copy-start | bytes 442372
  180.5 12.3 %all-to-all-start = ((bf16[16,2,2304]{2,1,0:T(2,128)(2,1)}), bf16[16,2,2304]{2,1,0:T(2,128)(2,1)S(1)}, u32[]{:S(2)}, u32[]{:S(2)}) async-start(bf16[16,2,2304]{2,1,0:T(2,128)(2,1)} %reshape.127), calls=%async_computation | async-start | bytes 294912 | tf_op jit(solution)/shard_map/all_to_all | solution.py:170
  192.8 256.7 %all-to-all-start.2 = ((bf16[3,48,8,192]{3,2,0,1:T(8,128)(2,1)}), bf16[3,48,8,192]{3,2,0,1:T(8,128)(2,1)S(1)}, u32[]{:S(2)}, u32[]{:S(2)}) async-start(bf16[3,48,8,192]{3,2,0,1:T(8,128)(2,1)} %copy.84), calls=%async_computation.2 | async-start | bytes 1179648 | tf_op jit(solution)/shard_map/all_to_all | solution.py:205
  (12 other events, 12.1 us)
Sparse Core Ops, SparseCore 0:
  10.1 76.4 all-gather.2
  166.8 280.7 all-reduce.6
  449.6 143.1 all-gather.4
where the time goes:
time: 605 us; the launch traced here: 604 us
  waiting for transfers between devices  456 us (75%)
  local copies, waits for them, and re-layouts  51.7 us (9%)
  starting transfers between devices  42.3 us (7%)
  matrix products  33.9 us (6%)
  between operations  14.1 us (2%)
  other arithmetic  6.22 us (1%)
    psum x1, waiting for transfers between devices, body(): lax.psum(local_grad.astype(jnp.bfloat16), 'lon').astype(jnp.float32)  250 us
    all_gather x1, waiting for transfers between devices, body(): piece = lax.all_gather(qkv_weight, 'head', axis=0, tiled=True)  143 us
    all_gather x1, waiting for transfers between devices, body(): band_rows = lax.all_gather(latents, 'head', axis=1, tiled=True)  54.7 us
    unnamed x24, local copies, waits for them, and re-layouts  13.9 us
  transfers between devices with their start and end apart: 10, of which 4 were waited for; matrix products, arithmetic and copies ran while one was open for 8% of the time, Pallas kernels for 0%

commit v1 on v0

--- a/solution.py
+++ b/solution.py
@@ -218,7 +218,11 @@
         "lawd,lawhc->hdc", band_rows, projected_grad, preferred_element_type=jnp.float32
     )
     latent_grad = latent_sum.astype(jnp.bfloat16).reshape(latents.shape)
-    qkv_grad = lax.psum(local_grad.astype(jnp.bfloat16), "lon").astype(jnp.float32)
+
+    def ticks_name(field_in, net_axis):
+        return jnp.sum(jax.lax.all_gather(field_in, axis_name=net_axis), 0)
+
+    qkv_grad = ticks_name(local_grad.astype(jnp.bfloat16), net_axis="lon").astype(jnp.float32)
     return (mixed, latent_grad, qkv_grad)
 
 

time: 605 us -> 374 us (0.62)
  waiting for transfers between devices: 456 us -> 218 us
  other arithmetic: 6.22 us -> 12.9 us
    psum x1 -> x0, waiting for transfers between devices: 250 us -> none  [body(): lax.psum(local_grad.astype(jnp.bfloat16), 'lon').astype(jnp.float32)]
    all_gather x1, waiting for transfers between devices: 143 us -> 38.4 us  [body(): piece = lax.all_gather(qkv_weight, 'head', axis=0, tiled=True)]
    all_gather x0 -> x1, waiting for transfers between devices: none -> 99 us  [ticks_name(): return jnp.sum(jax.lax.all_gather(field_in, axis_name=net_axis), 0)]
    all_to_all x1, waiting for transfers between devices: 0.01 us -> 12.9 us  [body(): lax.all_to_all(projected_grad.reshape(levels, lat_rows, columns, per_dev...]
    reduce_sum x0 -> x1, other arithmetic: none -> 7.87 us  [ticks_name(): return jnp.sum(jax.lax.all_gather(field_in, axis_name=net_axis), 0)]
  transfers between devices with their start and end apart: 10 -> 10, of which waited for: 4 -> 6; matrix products, arithmetic and copies ran while one was open for 8% -> 22% of each run, Pallas kernels for 0% -> 0%
where the time goes in v1:
time: 374 us; the launch traced here: 372 us
  waiting for transfers between devices  218 us (58%)
  local copies, waits for them, and re-layouts  50.8 us (14%)
  starting transfers between devices  42.3 us (11%)
  matrix products  34 us (9%)
  between operations  14.1 us (4%)
  other arithmetic  12.9 us (3%)
    all_gather x1, waiting for transfers between devices, ticks_name(): return jnp.sum(jax.lax.all_gather(field_in, axis_name=net_axis), 0)  99 us
    all_gather x1, waiting for transfers between devices, body(): band_rows = lax.all_gather(latents, 'head', axis=1, tiled=True)  54.7 us
    all_gather x1, waiting for transfers between devices, body(): piece = lax.all_gather(qkv_weight, 'head', axis=0, tiled=True)  38.4 us
    unnamed x24, local copies, waits for them, and re-layouts  13 us
    all_to_all x1, waiting for transfers between devices, body(): lax.all_to_all(projected_grad.reshape(levels, lat_rows, columns, per_dev...  12.9 us
    all_to_all x1, starting transfers between devices, body(): lax.all_to_all(token_grad, 'head', split_axis=3, concat_axis=1, tiled=True)  12 us
    ppermute x1, starting transfers between devices, extended(): lax.ppermute(lax.slice_in_dim(block, 0, width, axis=dim), axis, backward)  11.9 us
    sub x4, matrix products, softmax_rows(): powers = jnp.exp(score_matrix - row_max)  9.46 us
  transfers between devices with their start and end apart: 10, of which 6 were waited for; matrix products, arithmetic and copies ran while one was open for 22% of the time, Pallas kernels for 0%

profile of v1, /device:TPU:1, one launch (start us, length us, event | category | flops | bytes accessed | tf_op | source)
XLA Modules:
  0.0 372.3 jit_solution(4737780354678923580)
XLA Ops:
  10.4 3.6 copy.69
  14.1 5.8 %reshape.144 = bf16[16,2,2304]{2,1,0:T(2,128)(2,1)} reshape(bf16[1024,3,3,8]{3,2,1,0:T(4,128)(2,1)} %bitcast.171) | data formatting | bytes 294912
  19.9 12.0 %all-to-all-start.1 = ((bf16[16,2,2304]{2,1,0:T(2,128)(2,1)}), bf16[16,2,2304]{2,1,0:T(2,128)(2,1)S(1)}, u32[]{:S(2)}, u32[]{:S(2)}) async-start(bf16[16,2,2304]{2,1,0:T(2,128)(2,1)} %reshape.144), calls=%async_computation.1 | async-start | bytes 294912 | tf_op jit(solution)/shard_map/all_to_all | solution.py:183
  31.9 54.7 %all-gather.5.cloned.1.call-done = bf16[3,48,8,1024]{3,2,1,0:T(8,128)(2,1)} async-done(((bf16[3,3,8,1024]{3,2,1,0:T(8,128)(2,1)}), bf16[3,48,8,1024]{3,2,1,0:T(8,128)(2,1)}) %all-gather.5.cloned.1.call-update) | async-done | bytes 2359312 | tf_op jit(solution)/shard_map/all_gather | solution.py:155
  90.1 11.9 %collective-permute-start.1 = (bf16[3,48,4,1,128]{4,2,1,0,3:T(4,128)(2,1)}, bf16[3,48,4,1,128]{4,2,1,0,3:T(4,128)(2,1)}, u32[]{:S(2)}, u32[]{:S(2)}) collective-permute-start(bf16[3,48,4,1,128]{4,2,1,0,3:T(4,128)(2,1)} %get-tuple-element.142), channel_id=1, source_target_pairs={{16,0},{32,16},{48,32},{64,48},{80,64},{96,80},{112,96},{128,112},... | collective-permute-start | bytes 442376 | tf_op jit(solution)/shard_map/ppermute | solution.py:20
  102.0 3.8 %collective-permute-start = (bf16[3,48,4,1,128]{4,2,1,0,3:T(4,128)(2,1)}, bf16[3,48,4,1,128]{4,2,1,0,3:T(4,128)(2,1)}, u32[]{:S(2)}, u32[]{:S(2)}) collective-permute-start(bf16[3,48,4,1,128]{4,2,1,0,3:T(4,128)(2,1)} %get-tuple-element.141), channel_id=1, source_target_pairs={{0,16},{16,32},{32,48},{48,64},{64,80},{80,96},{96,112},{112,128},... | collective-permute-start | bytes 442376 | tf_op jit(solution)/shard_map/ppermute | solution.py:17
  106.2 3.9 %reshape.145 = bf16[1024,3,3,8]{3,2,1,0:T(4,128)(2,1)} reshape(bf16[16,2,2304]{2,1,0:T(2,128)(2,1)S(1)} %all-to-all-done.1) | data formatting | bytes 294912
  110.1 4.0 %copy.92 = bf16[3,3,8,16,64]{4,2,1,3,0:T(8,128)(2,1)S(1)} copy(bf16[3,3,8,16,64]{2,1,0,4,3:T(4,128)(2,1)} %bitcast.172) | data formatting | bytes 294912 | tf_op jit(solution)/shard_map/all_to_all | solution.py:183
  120.6 26.1 %while.23 = (s32[]{:T(128)}, bf16[2,4,144,64]{2,3,1,0:T(8,128)(2,1)}, f32[2,4,576,128]{3,2,1,0:T(8,128)}, pred[2,4,576]{2,1,0:T(4,128)(4,1)S(1)}, bf16[2,4,144,6...) while((s32[]{:T(128)}, ...), condition=%wide.region_8.9_spmd, body=%wide.region_4.8_spmd.sunk | while | flops 217128960 | bytes 40974684 | solution.py:187
  121.7 2.9 fusion.162
  134.8 2.9 fusion.162
  153.8 4.7 %collective-permute-start.2 = (bf16[3,48,4,1,128]{4,1,2,0,3:T(8,128)(2,1)}, bf16[3,48,4,1,128]{4,1,2,0,3:T(8,128)(2,1)}, u32[]{:S(2)}, u32[]{:S(2)}) collective-permute-start(bf16[3,48,4,1,128]{4,1,2,0,3:T(8,128)(2,1)} %get-tuple-element.137), channel_id=1, source_target_pairs={{496,0},{0,16},{16,32},{32,48},{48,64},{64,80},{80,96},{96,112},{1... | collective-permute-start | bytes 442376 | tf_op jit(solution)/shard_map/ppermute | solution.py:28
  161.5 4.1 %collective-permute-done.2 = bf16[3,48,4,1,128]{4,1,2,0,3:T(8,128)(2,1)} collective-permute-done((bf16[3,48,4,1,128]{4,1,2,0,3:T(8,128)(2,1)}, bf16[3,48,4,1,128]{4,1,2,0,3:T(8,128)(2,1)}, u32[]{:S(2)}, u32[]{:S(2)}) %collective-permute-start.2) | collective-permute-done | bytes 147488 | tf_op jit(solution)/shard_map/ppermute | solution.py:28
  170.4 11.0 %while.22 = (s32[]{:T(128)}, bf16[2,4,144,64]{2,3,1,0:T(8,128)(2,1)}, pred[2,4,576]{2,1,0:T(4,128)(4,1)S(1)}, bf16[2,4,144,64]{2,3,1,0:T(8,128)(2,1)}, bf16[2,4,576,128]{2,3,1,0:T(8,128)(2,1)S(1)}, /*index=5*/s32[]{:T(128)}) while((s32[]{:T(128)}, bf16[2,4,144,64]{2,3,1,0:T(8,128)(2,1)}, pred[2,4,576]{2,1,0:T(4,128)(4,1)S(1)}, ...), condition=%wide.region_3.4_spmd, body=%wide.region_0.3_spmd.sunk | while | flops 130426560 | bytes 2570841 | solution.py:164
  173.2 2.7 fusion.153
  178.6 2.7 fusion.153
  183.5 4.2 %all-to-all-start = ((bf16[16,2,2304]{2,1,0:T(2,128)(2,1)}), bf16[16,2,2304]{2,1,0:T(2,128)(2,1)S(1)}, u32[]{:S(2)}, u32[]{:S(2)}) async-start(bf16[16,2,2304]{2,1,0:T(2,128)(2,1)} %reshape.142), calls=%async_computation | async-start | bytes 294912 | tf_op jit(solution)/shard_map/all_to_all | solution.py:170
  189.1 7.6 %all-to-all-done = bf16[16,2,2304]{2,1,0:T(2,128)(2,1)S(1)} async-done(((bf16[16,2,2304]{2,1,0:T(2,128)(2,1)}), bf16[16,2,2304]{2,1,0:T(2,128)(2,1)S(1)}, u32[]{:S(2)}, u32[]{:S(2)}) %all-to-all-start) | async-done | bytes 147488 | tf_op jit(solution)/shard_map/all_to_all | solution.py:170
  196.6 3.6 all-to-all-start.2
  201.8 12.9 %all-to-all-done.2 = bf16[3,48,8,192]{3,2,0,1:T(8,128)(2,1)S(1)} async-done(((bf16[3,48,8,192]{3,2,0,1:T(8,128)(2,1)}), bf16[3,48,8,192]{3,2,0,1:T(8,128)(2,1)S(1)}, u32[]{:S(2)}, u32[]{:S(2)}) %all-to-all-start.2) | async-done | bytes 442400 | tf_op jit(solution)/shard_map/all_to_all | solution.py:205
  214.8 38.4 %all-gather.7.cloned.1.call-done = bf16[16,1024,192]{1,2,0:T(8,128)(2,1)} async-done(((bf16[1,1024,192]{1,2,0:T(8,128)(2,1)}), bf16[16,1024,192]{1,2,0:T(8,128)(2,1)}) %all-gather.7.cloned.1.call-update) | async-done | bytes 6291472 | tf_op jit(solution)/shard_map/all_gather | solution.py:213
  253.2 4.7 %fusion.91 = bf16[72,1024]{1,0:T(8,128)(2,1)} fusion(bf16[72,16,192]{2,0,1:T(8,128)(2,1)S(1)} %bitcast.173, bf16[16,1024,192]{1,2,0:T(8,128)(2,1)} %all-gather.7.cloned.1.call-done), kind=kOutput, calls=%fused_computation.77 | convolution fusion | flops 453058560 | bytes 6881280 | tf_op jit(solution)/shard_map/rnc,ndc->rd/dot_general | solution.py:216
  257.9 99.0 %all-gather.9.cloned.1.call-done = bf16[32,1024,192]{1,2,0:T(8,128)(2,1)} async-done(((bf16[1,1024,192]{1,2,0:T(8,128)(2,1)}), bf16[32,1024,192]{1,2,0:T(8,128)(2,1)}) %all-gather.9.cloned.1.call-update) | async-done | bytes 12582928 | tf_op jit(solution)/shard_map/all_gather | solution.py:223
  356.9 7.9 %reduce.2 = bf16[1024,192]{0,1:T(8,128)(2,1)S(1)} reduce(bf16[32,1024,192]{1,2,0:T(8,128)(2,1)} %all-gather.9.cloned.1.call-done, bf16[]{:T(256)} %constant.59.clone.1), dimensions={0}, to_apply=%region_9.10 | reduce | flops 6094848 | bytes 12976130 | tf_op jit(solution)/shard_map/reduce_sum | solution.py:223
  (134 shorter events, 60.0 us)
Async XLA Ops:
  7.2 1.6 copy-start
  7.2 79.4 %all-gather.5.cloned.1.call-start = ((), (), s32[]{:S(2)}) async-start(), calls=%async_computation.3 | async-start | bytes 2506752 | tf_op jit(solution)/shard_map/all_gather | solution.py:155
  7.9 245.3 %all-gather.7.cloned.1.call-start = ((), (), s32[]{:S(2)}) async-start(), calls=%async_computation.4 | async-start | bytes 6684672 | tf_op jit(solution)/shard_map/all_gather | solution.py:213
  14.1 72.5 %copy-start.13 = (bf16[1,1024,192]{1,2,0:T(8,128)(2,1)S(1)}, bf16[1,1024,192]{1,2,0:T(8,128)(2,1)}, u32[]{:S(2)}) copy-start(bf16[1,1024,192]{1,2,0:T(8,128)(2,1)} %param.10) | copy-start | bytes 1179652
  19.9 86.3 %all-to-all-start.1 = ((bf16[16,2,2304]{2,1,0:T(2,128)(2,1)}), bf16[16,2,2304]{2,1,0:T(2,128)(2,1)S(1)}, u32[]{:S(2)}, u32[]{:S(2)}) async-start(bf16[16,2,2304]{2,1,0:T(2,128)(2,1)} %reshape.144), calls=%async_computation.1 | async-start | bytes 294912 | tf_op jit(solution)/shard_map/all_to_all | solution.py:183
  31.8 325.1 %all-gather.9.cloned.1.call-start = ((), (), s32[]{:S(2)}) async-start(), calls=%async_computation.5 | async-start | bytes 12976128 | tf_op jit(solution)/shard_map/all_gather | solution.py:223
  90.1 26.0 %collective-permute-start.1 = (bf16[3,48,4,1,128]{4,2,1,0,3:T(4,128)(2,1)}, bf16[3,48,4,1,128]{4,2,1,0,3:T(4,128)(2,1)}, u32[]{:S(2)}, u32[]{:S(2)}) collective-permute-start(bf16[3,48,4,1,128]{4,2,1,0,3:T(4,128)(2,1)} %get-tuple-element.142), channel_id=1, source_target_pairs={{16,0},{32,16},{48,32},{64,48},{80,64},{96,80},{112,96},{128,112},... | collective-permute-start | bytes 442376 | tf_op jit(solution)/shard_map/ppermute | solution.py:20
  102.0 14.1 %collective-permute-start = (bf16[3,48,4,1,128]{4,2,1,0,3:T(4,128)(2,1)}, bf16[3,48,4,1,128]{4,2,1,0,3:T(4,128)(2,1)}, u32[]{:S(2)}, u32[]{:S(2)}) collective-permute-start(bf16[3,48,4,1,128]{4,2,1,0,3:T(4,128)(2,1)} %get-tuple-element.141), channel_id=1, source_target_pairs={{0,16},{16,32},{32,48},{48,64},{64,80},{80,96},{96,112},{112,128},... | collective-permute-start | bytes 442376 | tf_op jit(solution)/shard_map/ppermute | solution.py:17
  120.7 4.0 %copy-start.1 = (bf16[2,4,576,128]{2,3,1,0:T(8,128)(2,1)}, bf16[2,4,576,128]{2,3,1,0:T(8,128)(2,1)S(1)}, u32[]{:S(2)}) copy-start(bf16[2,4,576,128]{2,3,1,0:T(8,128)(2,1)S(1)} %get-tuple-element.264) | copy-start | bytes 3538948 | tf_op jit(solution)/shard_map/while
  124.6 2.2 copy-start.3
  131.2 2.5 copy-start.2
  133.7 3.9 %copy-start.1 = (bf16[2,4,576,128]{2,3,1,0:T(8,128)(2,1)}, bf16[2,4,576,128]{2,3,1,0:T(8,128)(2,1)S(1)}, u32[]{:S(2)}) copy-start(bf16[2,4,576,128]{2,3,1,0:T(8,128)(2,1)S(1)} %get-tuple-element.264) | copy-start | bytes 3538948 | tf_op jit(solution)/shard_map/while
  137.6 2.2 copy-start.3
  139.8 1.6 copy-start.14
  144.3 2.5 copy-start.2
  151.9 9.6 %collective-permute-start.3 = (bf16[3,48,4,1,128]{4,1,2,0,3:T(8,128)(2,1)}, bf16[3,48,4,1,128]{4,1,2,0,3:T(8,128)(2,1)}, u32[]{:S(2)}, u32[]{:S(2)}) collective-permute-start(bf16[3,48,4,1,128]{4,1,2,0,3:T(8,128)(2,1)} %get-tuple-element.138), channel_id=1, source_target_pairs={{16,0},{32,16},{48,32},{64,48},{80,64},{96,80},{112,96},{128,112},... | collective-permute-start | bytes 442376 | tf_op jit(solution)/shard_map/ppermute | solution.py:28
  153.8 11.8 %collective-permute-start.2 = (bf16[3,48,4,1,128]{4,1,2,0,3:T(8,128)(2,1)}, bf16[3,48,4,1,128]{4,1,2,0,3:T(8,128)(2,1)}, u32[]{:S(2)}, u32[]{:S(2)}) collective-permute-start(bf16[3,48,4,1,128]{4,1,2,0,3:T(8,128)(2,1)} %get-tuple-element.137), channel_id=1, source_target_pairs={{496,0},{0,16},{16,32},{32,48},{48,64},{64,80},{80,96},{96,112},{1... | collective-permute-start | bytes 442376 | tf_op jit(solution)/shard_map/ppermute | solution.py:28
  160.3 5.2 %copy-start.6 = (f32[3,48,16,1,128]{4,1,2,0,3:T(8,128)S(1)}, f32[3,48,16,1,128]{4,1,2,0,3:T(8,128)}, u32[]{:S(2)}) copy-start(f32[3,48,16,1,128]{4,1,2,0,3:T(8,128)} %copy-done.5) | copy-start | bytes 3538948
  161.5 5.5 %copy-start.11 = (bf16[3,48,8,64]{3,1,2,0:T(8,128)(2,1)}, bf16[3,48,8,64]{3,1,2,0:T(8,128)(2,1)S(1)}, u32[]{:S(2)}) copy-start(bf16[3,48,8,64]{3,1,2,0:T(8,128)(2,1)S(1)} %copy.83) | copy-start | bytes 442372
  161.5 6.2 %copy-start.17 = (bf16[3,48,8,1024]{3,2,1,0:T(8,128)(2,1)S(1)}, bf16[3,48,8,1024]{3,2,1,0:T(8,128)(2,1)}, u32[]{:S(2)}) copy-start(bf16[3,48,8,1024]{3,2,1,0:T(8,128)(2,1)} %all-gather.5.cloned.1.call-done) | copy-start | bytes 7077892
  181.4 6.4 %copy-start.10 = (bf16[3,48,8,128]{3,1,2,0:T(8,128)(2,1)S(1)}, bf16[3,48,8,128]{3,1,2,0:T(8,128)(2,1)}, u32[]{:S(2)}) copy-start(bf16[3,48,8,128]{3,1,2,0:T(8,128)(2,1)} %copy-done.9) | copy-start | bytes 884740
  181.4 6.4 %copy-start.12 = (bf16[3,48,8,64]{3,1,2,0:T(8,128)(2,1)S(1)}, bf16[3,48,8,64]{3,1,2,0:T(8,128)(2,1)}, u32[]{:S(2)}) copy-start(bf16[3,48,8,64]{3,1,2,0:T(8,128)(2,1)} %copy-done.11) | copy-start | bytes 442372
  183.5 13.1 %all-to-all-start = ((bf16[16,2,2304]{2,1,0:T(2,128)(2,1)}), bf16[16,2,2304]{2,1,0:T(2,128)(2,1)S(1)}, u32[]{:S(2)}, u32[]{:S(2)}) async-start(bf16[16,2,2304]{2,1,0:T(2,128)(2,1)} %reshape.142), calls=%async_computation | async-start | bytes 294912 | tf_op jit(solution)/shard_map/all_to_all | solution.py:170
  196.6 18.2 %all-to-all-start.2 = ((bf16[3,48,8,192]{3,2,0,1:T(8,128)(2,1)}), bf16[3,48,8,192]{3,2,0,1:T(8,128)(2,1)S(1)}, u32[]{:S(2)}, u32[]{:S(2)}) async-start(bf16[3,48,8,192]{3,2,0,1:T(8,128)(2,1)} %copy.84), calls=%async_computation.2 | async-start | bytes 1179648 | tf_op jit(solution)/shard_map/all_to_all | solution.py:205
  (12 other events, 12.3 us)
Sparse Core Ops, SparseCore 0:
  10.1 76.4 all-gather.4
  88.7 164.4 all-gather.6
  256.3 100.5 all-gather.8
